TPU v7x, 32 devices: a whole 2x2x4 slice. The times are simulated.
32 devices in a mesh: tm: 16 (over z, y, core), strip: 2 (over x).
Axes of the slice: x: 2, y: 2, z: 4, core: 2. Of those that a mesh axis runs over, the one named last changes fastest.
Arguments:
- forward_u: float32 [16, 128, 1024], P('tm', 'strip'), may hold values from -4 to 4
- forward_v: float32 [16, 128, 1024], P('tm', 'strip'), may hold values from -4 to 4
- permittivity: float32 [128, 1024], P('strip'), may hold values from 1 to 3
- coarse_rate: float32 [16, 128, 1024], P('tm', 'strip'), may hold values from 0.2 to 8
- modulation: float32 [32], replicated, may hold values from 0 to 0.3
- tile_map: int32 [1, 8], replicated, may hold values from 0 to 31
- start_step: int32 [16], P('tm'), may hold values from 0 to 255
Outputs:
- adjoint_u: float32 [16, 128, 1024], P('tm', 'strip')
- adjoint_v: float32 [16, 128, 1024], P('tm', 'strip')
- depth_grad: float32 [32], replicated
Inputs may be any that keep to these rules, and one draw needn't show every extreme that they name: `tile_map`: tile parameter indices. `start_step`: start steps within one period.
All inputs are finite; a program needn't handle non-finite values.
Results may differ from a plain program's by a relative error of at most 0.0003.
Values sent between devices are 32-bit elements; how exact they have to be, the bound alone decides.
A program may use at most 128 MiB of HBM per device.

v0:
```python
import jax
import jax.numpy as jnp
from jax import lax
from jax.sharding import PartitionSpec as P

TILE = 128
STEPS = 2
STENCIL = 4
PERIOD = 256
stencil_coef = (-205.0 / 72.0, 8.0 / 5.0, -1.0 / 5.0, 8.0 / 315.0, -1.0 / 560.0)
time_step = 0.4
damping_rate = 0.1


def padded_2(cells, sides, width):
    for axis, dim in sides:
        count = lax.axis_size(axis)
        ends = count - 1
        head = lax.slice_in_dim(cells, 0, width, axis=dim)
        tail = lax.slice_in_dim(cells, cells.shape[dim] - width, cells.shape[dim], axis=dim)
        cells = jnp.concatenate(
            [
                lax.ppermute(tail, axis, [(i, (i + 1) % count) for i in range(ends)]),
                cells,
                lax.ppermute(head, axis, [((i + 1) % count, i) for i in range(ends)]),
            ],
            axis=dim,
        )
    return cells


def from_behind(array, axis, by):
    length = lax.axis_size(axis)
    return lax.ppermute(array, axis, [(i, (i + by) % length) for i in range(length)])


def entering(part, axis, combine, identity, reverse):
    count = lax.axis_size(axis)
    place = lax.axis_index(axis)
    ahead = count - 1 - place if reverse else place
    gathered = jax.tree.map(lambda a: lax.all_gather(a, axis), part)
    state = jax.tree.map(lambda a, e: jnp.zeros_like(a) + jnp.asarray(e, a.dtype), part, identity)

    def one(turn, state):
        source = count - 1 - turn if reverse else turn
        return combine(
            state, jax.tree.map(lambda a: lax.dynamic_index_in_dim(a, source, 0, False), gathered)
        )

    return lax.fori_loop(0, ahead, one, state)


def laplacian_rows(padded, rim_width):
    row_count = padded.shape[0] - 2 * rim_width
    center = padded[rim_width : rim_width + row_count]
    summed = 2.0 * stencil_coef[0] * center
    for offset in range(1, 5):
        along_x = (
            padded[rim_width + offset : rim_width + offset + row_count]
            + padded[rim_width - offset : rim_width - offset + row_count]
        )
        along_y = jnp.roll(center, offset, axis=1) + jnp.roll(center, -offset, axis=1)
        summed = summed + stencil_coef[offset] * (along_x + along_y)
    return summed


def row_selector(first_row, row_count, tile_rows):
    global_rows = first_row + jnp.arange(row_count, dtype=jnp.int32)
    tile_index = global_rows // TILE
    return (tile_index[:, None] == jnp.arange(tile_rows, dtype=jnp.int32)[None, :]).astype(
        jnp.float32
    )


def rows_depth(first_row, row_count, tile_depth):
    selector = row_selector(first_row, row_count, tile_depth.shape[0])
    per_tile = jnp.dot(selector, tile_depth, precision=lax.Precision.HIGHEST)
    return jnp.repeat(per_tile, TILE, axis=1)


def compose_high(earlier, latter):
    return (latter[0] * earlier[0], latter[0][None] * earlier[1] + latter[1])


def compose_low(earlier, latter):
    return (earlier[0] * latter[0], earlier[0][None] * latter[1] + earlier[1])


def shards(forward_u, forward_v, permittivity, coarse_rate, modulation, tile_map, start_step):
    start_u = forward_u[0]
    start_v = forward_v[0]
    strip_rows = start_u.shape[0]
    strip_place = lax.axis_index("strip")
    slice_count = lax.axis_size("tm")
    selector_params = (
        tile_map[:, :, None] == jnp.arange(modulation.shape[0], dtype=jnp.int32)[None, None, :]
    ).astype(jnp.float32)
    tile_depth = jnp.sum(selector_params * modulation[None, None, :], axis=2)
    cell_depth = rows_depth(strip_place * strip_rows, strip_rows, tile_depth)
    offsets = (start_step[0] + jnp.arange(STEPS, dtype=jnp.int32)).astype(jnp.float32)
    cosines = jnp.cos(2.0 * jnp.pi / PERIOD * offsets)
    eps_list = [permittivity * (1.0 + cell_depth * cosines[level]) for level in range(STEPS)]
    forcings = []
    field_u = start_u
    field_v = start_v
    for level in range(STEPS):
        padded = padded_2(field_u, (("strip", 0),), STENCIL)
        forcing = laplacian_rows(padded, STENCIL) - damping_rate * field_v
        forcings.append(forcing)
        field_v = field_v + time_step * forcing / eps_list[level]
        field_u = field_u + time_step * field_v
    following = from_behind(jnp.stack([start_u, start_v]), "tm", -1)
    mismatch = jnp.stack([field_u, field_v]) - following
    retain = jnp.exp(-coarse_rate[0] / slice_count)
    ones = jnp.ones_like(retain)
    zeros = jnp.zeros_like(mismatch)
    higher_a, higher_b = entering((retain, mismatch), "tm", compose_high, (ones, zeros), True)
    lower_a, lower_b = entering((retain, mismatch), "tm", compose_low, (ones, zeros), False)
    cycle_a = retain * higher_a * lower_a
    cycle_b = retain[None] * (higher_a[None] * lower_b + higher_b) + mismatch
    coarse = cycle_b / (1.0 - cycle_a)[None]
    preceding = from_behind(coarse, "tm", 1)
    gradient_cells = jnp.zeros_like(start_u)
    back_u = coarse[0]
    back_v = coarse[1]
    for level in reversed(range(STEPS)):
        eps_now = eps_list[level]
        total_v = back_v + time_step * back_u
        weighted = time_step / eps_now * total_v
        padded = padded_2(weighted, (("strip", 0),), STENCIL)
        back_u = back_u + laplacian_rows(padded, STENCIL)
        back_v = (1.0 - time_step * damping_rate / eps_now) * total_v
        gradient_cells = gradient_cells - cosines[level] * time_step * total_v * forcings[level] / (
            eps_now * eps_now
        )
    cell_terms = gradient_cells * permittivity
    column_sums = jnp.sum(cell_terms.reshape(strip_rows, cell_terms.shape[1] // TILE, TILE), axis=2)
    selector = row_selector(strip_place * strip_rows, strip_rows, tile_map.shape[0])
    tile_part = jnp.dot(selector.T, column_sums, precision=lax.Precision.HIGHEST)
    param_part = jnp.sum(selector_params * tile_part[:, :, None], axis=(0, 1))
    depth_grad = lax.psum(param_part, ("tm", "strip"))
    adjoint_u = back_u - preceding[0]
    adjoint_v = back_v - preceding[1]
    return (adjoint_u[None], adjoint_v[None], depth_grad)


def solution(mesh):
    placed = (
        P("tm", "strip", None),
        P("tm", "strip", None),
        P("strip", None),
        P("tm", "strip", None),
        P(),
        P(),
        P("tm"),
    )
    return jax.shard_map(
        shards,
        mesh=mesh,
        in_specs=placed,
        out_specs=(P("tm", "strip", None), P("tm", "strip", None), P()),
        check_vma=False,
    )
```

profile of v0, /device:TPU:0, one launch (start us, length us, event | category | flops | bytes accessed | tf_op | source)
XLA Modules:
  0.0 250.6 jit_solution(9343302233114372609)
XLA Ops:
  7.2 1.8 fusion.108
  9.9 4.9 %collective-permute-start.1 = (f32[4,1024]{1,0:T(4,128)S(1)}, f32[4,1024]{1,0:T(4,128)S(1)}, u32[]{:S(2)}, u32[]{:S(2)}) collective-permute-start(f32[4,1024]{1,0:T(4,128)S(1)} %get-tuple-element.229), channel_id=1, source_target_pairs={{0,1},{2,3},{4,5},{6,7},{8,9},{10,11},{12,13},{14,15},{16,17},{18,... | collective-permute-start | bytes 49160 | tf_op jit(solution)/shard_map/ppermute | solution.py:23
  14.7 1.3 collective-permute-start
  16.0 1.9 pad_maximum_fusion
  17.9 3.7 %collective-permute-start.4 = (f32[2,64,1024]{2,1,0:T(8,128)}, f32[2,64,1024]{2,1,0:T(8,128)S(1)}, u32[]{:S(2)}, u32[]{:S(2)}) collective-permute-start(f32[2,64,1024]{2,1,0:T(8,128)} %pad_maximum_fusion), channel_id=1, source_target_pairs={{0,30},{2,0},{4,2},{6,4},{8,6},{10,8},{12,10},{14,12},{16,14},{18,... | collective-permute-start | bytes 1572872 | tf_op jit(solution)/shard_map/ppermute | solution.py:34
  31.9 1.3 fusion.99
  33.5 4.0 %multiply_add_fusion.1 = (f32[64,1024]{1,0:T(8,128)S(1)}, f32[64,1024]{1,0:T(8,128)S(1)}, f32[64,1024]{1,0:T(8,128)}, f32[64,1024]{1,0:T(8,128)S(1)}) fusion(f32[1,64,1024]{2,1,0:T(8,128)} %param.11, f32[1,64,1024]{2,1,0:T(8,128)} %param.12, f32[64,4]{1,0:T(8,128)S(1)} %get-tuple-element.231, f32[64,1020]{1,0:T(8,128)S(1)} %get-tuple-element.233, ...), kind=kLoop, calls=%fused_computation.193 | loop fusion | flops 2949120 | bytes 4489216 | tf_op jit(solution)/shard_map/add | solution.py:111
  37.5 4.3 %collective-permute-start.3 = (f32[4,1024]{1,0:T(4,128)S(1)}, f32[4,1024]{1,0:T(4,128)S(1)}, u32[]{:S(2)}, u32[]{:S(2)}) collective-permute-start(f32[4,1024]{1,0:T(4,128)S(1)} %get-tuple-element.211), channel_id=1, source_target_pairs={{0,1},{2,3},{4,5},{6,7},{8,9},{10,11},{12,13},{14,15},{16,17},{18,... | collective-permute-start | bytes 49160 | tf_op jit(solution)/shard_map/ppermute | solution.py:23
  41.8 1.3 collective-permute-start.2
  43.9 3.5 %collective-permute-done.2 = f32[4,1024]{1,0:T(4,128)S(1)} collective-permute-done((f32[4,1024]{1,0:T(4,128)S(1)}, f32[4,1024]{1,0:T(4,128)S(1)}, u32[]{:S(2)}, u32[]{:S(2)}) %collective-permute-start.2) | collective-permute-done | bytes 16416 | tf_op jit(solution)/shard_map/ppermute | solution.py:25
  50.4 15.8 %all-gather.4.cloned.1.call-done = f32[16,64,1024]{2,1,0:T(8,128)} async-done(((f32[1,64,1024]{2,1,0:T(8,128)}), f32[16,64,1024]{2,1,0:T(8,128)}) %all-gather.4.cloned.1.call-update) | async-done | bytes 4194320 | tf_op jit(solution)/shard_map/all_gather | solution.py:41
  66.2 75.0 %all-gather.6.cloned.1.call-done = f32[32,64,1024]{2,1,0:T(8,128)} async-done(((f32[2,64,1024]{2,1,0:T(8,128)}), f32[32,64,1024]{2,1,0:T(8,128)}) %all-gather.6.cloned.1.call-update) | async-done | bytes 8388624 | tf_op jit(solution)/shard_map/all_gather | solution.py:41
  141.3 35.1 %while.26 = (s32[]{:T(128)}, f32[64,1024]{1,0:T(8,128)S(1)}, f32[2,64,1024]{2,1,0:T(8,128)S(1)}, s32[]{:T(128)}, f32[16,64,1024]{2,1,0:T(8,128)}, /*index=5*/f32...) while((s32[]{:T(128)}, f32[64,1024]{1,0:T(8,128)S(1)}, f32[2,64,1024]{2,1,0:T(8,128)S(1)}, ...), condition=%wide.region_2.3_spmd, body=%wide.region_1.2_spmd.sunk | while | flops 327686 | bytes 2883747 | solution.py:50
  147.0 1.3 bitcast_add_fusion.4
  177.4 1.4 add_divide_fusion
  179.7 3.4 %collective-permute-start.6 = (f32[4,1024]{1,0:T(4,128)S(1)}, f32[4,1024]{1,0:T(4,128)S(1)}, u32[]{:S(2)}, u32[]{:S(2)}) collective-permute-start(f32[4,1024]{1,0:T(4,128)S(1)} %get-tuple-element.191), channel_id=1, source_target_pairs={{0,1},{2,3},{4,5},{6,7},{8,9},{10,11},{12,13},{14,15},{16,17},{18,... | collective-permute-start | bytes 49160 | tf_op jit(solution)/shard_map/ppermute | solution.py:23
  183.0 1.3 collective-permute-start.5
  184.5 4.2 %collective-permute-done.5 = f32[4,1024]{1,0:T(4,128)S(1)} collective-permute-done((f32[4,1024]{1,0:T(4,128)S(1)}, f32[4,1024]{1,0:T(4,128)S(1)}, u32[]{:S(2)}, u32[]{:S(2)}) %collective-permute-start.5) | collective-permute-done | bytes 16416 | tf_op jit(solution)/shard_map/ppermute | solution.py:25
  189.8 39.4 %psum.7 = f32[32]{0:T(128)} all-reduce(f32[32]{0:T(128)S(1)} %select_reduce_fusion), channel_id=1, replica_groups=mesh['tm'=16,'strip'=2] {'tm','strip'}, use_global_device_ids=true, to_apply=%region_7.8 | all-reduce | flops 32 | bytes 256 | tf_op jit(solution)/shard_map/psum | solution.py:141
  229.2 1.7 fusion.84
  231.7 4.2 %collective-permute-start.8 = (f32[4,1024]{1,0:T(4,128)S(1)}, f32[4,1024]{1,0:T(4,128)S(1)}, u32[]{:S(2)}, u32[]{:S(2)}) collective-permute-start(f32[4,1024]{1,0:T(4,128)S(1)} %get-tuple-element.177), channel_id=1, source_target_pairs={{0,1},{2,3},{4,5},{6,7},{8,9},{10,11},{12,13},{14,15},{16,17},{18,... | collective-permute-start | bytes 49160 | tf_op jit(solution)/shard_map/ppermute | solution.py:23
  235.9 1.3 collective-permute-start.7
  237.3 4.2 %collective-permute-done.7 = f32[4,1024]{1,0:T(4,128)S(1)} collective-permute-done((f32[4,1024]{1,0:T(4,128)S(1)}, f32[4,1024]{1,0:T(4,128)S(1)}, u32[]{:S(2)}, u32[]{:S(2)}) %collective-permute-start.7) | collective-permute-done | bytes 16416 | tf_op jit(solution)/shard_map/ppermute | solution.py:25
  241.5 2.2 fusion.9
  (110 shorter events, 50.7 us)
Async XLA Ops:
  7.2 59.0 %all-gather.4.cloned.1.call-start = ((), (), s32[]{:S(2)}) async-start(), calls=%async_computation | async-start | bytes 4456448 | tf_op jit(solution)/shard_map/all_gather | solution.py:41
  9.0 38.5 %copy-start = (f32[64,1024]{1,0:T(8,128)S(1)}, f32[64,1024]{1,0:T(8,128)}, u32[]{:S(2)}) copy-start(f32[64,1024]{1,0:T(8,128)} %param.13) | copy-start | bytes 786436
  9.0 132.2 %all-gather.6.cloned.1.call-start = ((), (), s32[]{:S(2)}) async-start(), calls=%async_computation.1 | async-start | bytes 8912896 | tf_op jit(solution)/shard_map/all_gather | solution.py:41
  9.9 23.5 %collective-permute-start.1 = (f32[4,1024]{1,0:T(4,128)S(1)}, f32[4,1024]{1,0:T(4,128)S(1)}, u32[]{:S(2)}, u32[]{:S(2)}) collective-permute-start(f32[4,1024]{1,0:T(4,128)S(1)} %get-tuple-element.229), channel_id=1, source_target_pairs={{0,1},{2,3},{4,5},{6,7},{8,9},{10,11},{12,13},{14,15},{16,17},{18,... | collective-permute-start | bytes 49160 | tf_op jit(solution)/shard_map/ppermute | solution.py:23
  14.7 18.6 %collective-permute-start = (f32[4,1024]{1,0:T(4,128)S(1)}, f32[4,1024]{1,0:T(4,128)S(1)}, u32[]{:S(2)}, u32[]{:S(2)}) collective-permute-start(f32[4,1024]{1,0:T(4,128)S(1)} %get-tuple-element.228), channel_id=1, source_target_pairs={{1,0},{3,2},{5,4},{7,6},{9,8},{11,10},{13,12},{15,14},{17,16},{19,... | collective-permute-start | bytes 49160 | tf_op jit(solution)/shard_map/ppermute | solution.py:25
  17.9 30.3 %collective-permute-start.4 = (f32[2,64,1024]{2,1,0:T(8,128)}, f32[2,64,1024]{2,1,0:T(8,128)S(1)}, u32[]{:S(2)}, u32[]{:S(2)}) collective-permute-start(f32[2,64,1024]{2,1,0:T(8,128)} %pad_maximum_fusion), channel_id=1, source_target_pairs={{0,30},{2,0},{4,2},{6,4},{8,6},{10,8},{12,10},{14,12},{16,14},{18,... | collective-permute-start | bytes 1572872 | tf_op jit(solution)/shard_map/ppermute | solution.py:34
  37.5 6.4 %collective-permute-start.3 = (f32[4,1024]{1,0:T(4,128)S(1)}, f32[4,1024]{1,0:T(4,128)S(1)}, u32[]{:S(2)}, u32[]{:S(2)}) collective-permute-start(f32[4,1024]{1,0:T(4,128)S(1)} %get-tuple-element.211), channel_id=1, source_target_pairs={{0,1},{2,3},{4,5},{6,7},{8,9},{10,11},{12,13},{14,15},{16,17},{18,... | collective-permute-start | bytes 49160 | tf_op jit(solution)/shard_map/ppermute | solution.py:23
  41.8 5.6 %collective-permute-start.2 = (f32[4,1024]{1,0:T(4,128)S(1)}, f32[4,1024]{1,0:T(4,128)S(1)}, u32[]{:S(2)}, u32[]{:S(2)}) collective-permute-start(f32[4,1024]{1,0:T(4,128)S(1)} %get-tuple-element.210), channel_id=1, source_target_pairs={{1,0},{3,2},{5,4},{7,6},{9,8},{11,10},{13,12},{15,14},{17,16},{19,... | collective-permute-start | bytes 49160 | tf_op jit(solution)/shard_map/ppermute | solution.py:25
  48.2 93.0 %copy-start.1 = (f32[2,64,1024]{2,1,0:T(8,128)}, f32[2,64,1024]{2,1,0:T(8,128)S(1)}, u32[]{:S(2)}) copy-start(f32[2,64,1024]{2,1,0:T(8,128)S(1)} %collective-permute-done.4) | copy-start | bytes 1572868
  176.4 1.0 copy-start.3
  176.5 12.2 %copy-start.2 = (f32[64,1024]{1,0:T(8,128)S(1)}, f32[64,1024]{1,0:T(8,128)}, u32[]{:S(2)}) copy-start(f32[64,1024]{1,0:T(8,128)} %get-tuple-element.156) | copy-start | bytes 786436
  176.5 13.2 %copy-start.4 = (s32[1,8]{1,0:T(1,128)S(1)}, s32[1,8]{1,0:T(1,128)}, u32[]{:S(2)}) copy-start(s32[1,8]{1,0:T(1,128)} %param.16) | copy-start | bytes 100
  179.7 4.8 %collective-permute-start.6 = (f32[4,1024]{1,0:T(4,128)S(1)}, f32[4,1024]{1,0:T(4,128)S(1)}, u32[]{:S(2)}, u32[]{:S(2)}) collective-permute-start(f32[4,1024]{1,0:T(4,128)S(1)} %get-tuple-element.191), channel_id=1, source_target_pairs={{0,1},{2,3},{4,5},{6,7},{8,9},{10,11},{12,13},{14,15},{16,17},{18,... | collective-permute-start | bytes 49160 | tf_op jit(solution)/shard_map/ppermute | solution.py:23
  183.0 5.6 %collective-permute-start.5 = (f32[4,1024]{1,0:T(4,128)S(1)}, f32[4,1024]{1,0:T(4,128)S(1)}, u32[]{:S(2)}, u32[]{:S(2)}) collective-permute-start(f32[4,1024]{1,0:T(4,128)S(1)} %get-tuple-element.190), channel_id=1, source_target_pairs={{1,0},{3,2},{5,4},{7,6},{9,8},{11,10},{13,12},{15,14},{17,16},{19,... | collective-permute-start | bytes 49160 | tf_op jit(solution)/shard_map/ppermute | solution.py:25
  184.4 44.8 %collective-permute-start.9 = (f32[2,64,1024]{2,1,0:T(8,128)S(1)}, f32[2,64,1024]{2,1,0:T(8,128)}, u32[]{:S(2)}, u32[]{:S(2)}) collective-permute-start(f32[2,64,1024]{2,1,0:T(8,128)S(1)} %add_divide_fusion), channel_id=1, source_target_pairs={{0,2},{2,4},{4,6},{6,8},{8,10},{10,12},{12,14},{14,16},{16,18},{18... | collective-permute-start | bytes 1572872 | tf_op jit(solution)/shard_map/ppermute | solution.py:34
  231.7 5.6 %collective-permute-start.8 = (f32[4,1024]{1,0:T(4,128)S(1)}, f32[4,1024]{1,0:T(4,128)S(1)}, u32[]{:S(2)}, u32[]{:S(2)}) collective-permute-start(f32[4,1024]{1,0:T(4,128)S(1)} %get-tuple-element.177), channel_id=1, source_target_pairs={{0,1},{2,3},{4,5},{6,7},{8,9},{10,11},{12,13},{14,15},{16,17},{18,... | collective-permute-start | bytes 49160 | tf_op jit(solution)/shard_map/ppermute | solution.py:23
  235.9 5.6 %collective-permute-start.7 = (f32[4,1024]{1,0:T(4,128)S(1)}, f32[4,1024]{1,0:T(4,128)S(1)}, u32[]{:S(2)}, u32[]{:S(2)}) collective-permute-start(f32[4,1024]{1,0:T(4,128)S(1)} %get-tuple-element.176), channel_id=1, source_target_pairs={{1,0},{3,2},{5,4},{7,6},{9,8},{11,10},{13,12},{15,14},{17,16},{19,... | collective-permute-start | bytes 49160 | tf_op jit(solution)/shard_map/ppermute | solution.py:25
Sparse Core Ops, SparseCore 0:
  10.1 56.0 all-gather.3
  68.4 72.8 all-gather.5
where the time goes:
time: 253 us; the launch traced here: 251 us
  waiting for transfers between devices  103 us (41%)
  other arithmetic  52.5 us (21%)
  blocking collectives  39.4 us (16%)
  starting transfers between devices  25.6 us (10%)
  between operations  16.3 us (6%)
  local copies, waits for them, and re-layouts  13.4 us (5%)
    all_gather x2, waiting for transfers between devices, entering(): gathered = jax.tree.map(lambda a: lax.all_gather(a, axis), part)  90.8 us
    psum x1, blocking collectives, shards(): depth_grad = lax.psum(param_part, ('tm', 'strip'))  39.4 us
    add x15, other arithmetic, compose_high(): return (latter[0] * earlier[0], latter[0][None] * earlier[1] + latter[1])  19.3 us
    ppermute x4, starting transfers between devices, padded_2(): lax.ppermute(tail, axis, [(i, (i + 1) % count) for i in range(ends)])  16.7 us
    mul x15, other arithmetic, compose_high(): return (latter[0] * earlier[0], latter[0][None] * earlier[1] + latter[1])  15.4 us
    ppermute x4, waiting for transfers between devices, padded_2(): lax.ppermute(head, axis, [((i + 1) % count, i) for i in range(ends)])  11.9 us
    slice x24, local copies, waits for them, and re-layouts, laplacian_rows(): jnp.roll(center, offset, axis=1) + jnp.roll(center, -offset, axis=1)  9.75 us
    ppermute x4, starting transfers between devices, padded_2(): lax.ppermute(head, axis, [((i + 1) % count, i) for i in range(ends)])  5.17 us
  transfers between devices with their start and end apart: 12, of which 5 were waited for; matrix products, arithmetic and copies ran while one was open for 9% of the time, Pallas kernels for 0%

commit v1 on v0

--- a/solution.py
+++ b/solution.py
@@ -138,7 +138,9 @@
     selector = row_selector(strip_place * strip_rows, strip_rows, tile_map.shape[0])
     tile_part = jnp.dot(selector.T, column_sums, precision=lax.Precision.HIGHEST)
     param_part = jnp.sum(selector_params * tile_part[:, :, None], axis=(0, 1))
-    depth_grad = lax.psum(param_part, ("tm", "strip"))
+    depth_grad = param_part
+    for mesh_axis in ("tm", "strip"):
+        depth_grad = lax.psum(depth_grad, mesh_axis)
     adjoint_u = back_u - preceding[0]
     adjoint_v = back_v - preceding[1]
     return (adjoint_u[None], adjoint_v[None], depth_grad)

time: 253 us -> 249 us (0.984)
  blocking collectives: 39.4 us -> 35.7 us
    psum x1 -> x2, blocking collectives: 39.4 us -> 35.7 us  [shards(): depth_grad = lax.psum(depth_grad, mesh_axis)]
where the time goes in v1:
time: 249 us; the launch traced here: 247 us
  waiting for transfers between devices  103 us (41%)
  other arithmetic  52.5 us (21%)
  blocking collectives  35.7 us (14%)
  starting transfers between devices  25.4 us (10%)
  between operations  16.3 us (7%)
  local copies, waits for them, and re-layouts  13.4 us (5%)
    all_gather x2, waiting for transfers between devices, entering(): gathered = jax.tree.map(lambda a: lax.all_gather(a, axis), part)  90.8 us
    psum x2, blocking collectives, shards(): depth_grad = lax.psum(depth_grad, mesh_axis)  35.7 us
    add x15, other arithmetic, compose_high(): return (latter[0] * earlier[0], latter[0][None] * earlier[1] + latter[1])  19.3 us
    ppermute x4, starting transfers between devices, padded_2(): lax.ppermute(tail, axis, [(i, (i + 1) % count) for i in range(ends)])  16.4 us
    mul x15, other arithmetic, compose_high(): return (latter[0] * earlier[0], latter[0][None] * earlier[1] + latter[1])  15.4 us
    ppermute x4, waiting for transfers between devices, padded_2(): lax.ppermute(head, axis, [((i + 1) % count, i) for i in range(ends)])  11.9 us
    slice x24, local copies, waits for them, and re-layouts, laplacian_rows(): jnp.roll(center, offset, axis=1) + jnp.roll(center, -offset, axis=1)  9.75 us
    ppermute x4, starting transfers between devices, padded_2(): lax.ppermute(head, axis, [((i + 1) % count, i) for i in range(ends)])  5.17 us
  transfers between devices with their start and end apart: 12, of which 5 were waited for; matrix products, arithmetic and copies ran while one was open for 9% of the time, Pallas kernels for 0%

profile of v1, /device:TPU:0, one launch (start us, length us, event | category | flops | bytes accessed | tf_op | source)
XLA Modules:
  0.0 246.6 jit_solution(18319678654627542253)
XLA Ops:
  7.2 1.8 fusion.108
  9.9 4.9 %collective-permute-start.1 = (f32[4,1024]{1,0:T(4,128)S(1)}, f32[4,1024]{1,0:T(4,128)S(1)}, u32[]{:S(2)}, u32[]{:S(2)}) collective-permute-start(f32[4,1024]{1,0:T(4,128)S(1)} %get-tuple-element.229), channel_id=1, source_target_pairs={{0,1},{2,3},{4,5},{6,7},{8,9},{10,11},{12,13},{14,15},{16,17},{18,... | collective-permute-start | bytes 49160 | tf_op jit(solution)/shard_map/ppermute | solution.py:23
  14.7 1.3 collective-permute-start
  16.0 1.9 pad_maximum_fusion
  17.9 3.7 %collective-permute-start.4 = (f32[2,64,1024]{2,1,0:T(8,128)}, f32[2,64,1024]{2,1,0:T(8,128)S(1)}, u32[]{:S(2)}, u32[]{:S(2)}) collective-permute-start(f32[2,64,1024]{2,1,0:T(8,128)} %pad_maximum_fusion), channel_id=1, source_target_pairs={{0,30},{2,0},{4,2},{6,4},{8,6},{10,8},{12,10},{14,12},{16,14},{18,... | collective-permute-start | bytes 1572872 | tf_op jit(solution)/shard_map/ppermute | solution.py:34
  31.9 1.3 fusion.99
  33.5 4.0 %multiply_add_fusion.1 = (f32[64,1024]{1,0:T(8,128)S(1)}, f32[64,1024]{1,0:T(8,128)S(1)}, f32[64,1024]{1,0:T(8,128)}, f32[64,1024]{1,0:T(8,128)S(1)}) fusion(f32[1,64,1024]{2,1,0:T(8,128)} %param.11, f32[1,64,1024]{2,1,0:T(8,128)} %param.12, f32[64,4]{1,0:T(8,128)S(1)} %get-tuple-element.231, f32[64,1020]{1,0:T(8,128)S(1)} %get-tuple-element.233, ...), kind=kLoop, calls=%fused_computation.193 | loop fusion | flops 2949120 | bytes 4489216 | tf_op jit(solution)/shard_map/add | solution.py:111
  37.5 4.3 %collective-permute-start.3 = (f32[4,1024]{1,0:T(4,128)S(1)}, f32[4,1024]{1,0:T(4,128)S(1)}, u32[]{:S(2)}, u32[]{:S(2)}) collective-permute-start(f32[4,1024]{1,0:T(4,128)S(1)} %get-tuple-element.211), channel_id=1, source_target_pairs={{0,1},{2,3},{4,5},{6,7},{8,9},{10,11},{12,13},{14,15},{16,17},{18,... | collective-permute-start | bytes 49160 | tf_op jit(solution)/shard_map/ppermute | solution.py:23
  41.8 1.3 collective-permute-start.2
  44.0 3.5 %collective-permute-done.2 = f32[4,1024]{1,0:T(4,128)S(1)} collective-permute-done((f32[4,1024]{1,0:T(4,128)S(1)}, f32[4,1024]{1,0:T(4,128)S(1)}, u32[]{:S(2)}, u32[]{:S(2)}) %collective-permute-start.2) | collective-permute-done | bytes 16416 | tf_op jit(solution)/shard_map/ppermute | solution.py:25
  50.4 15.8 %all-gather.4.cloned.1.call-done = f32[16,64,1024]{2,1,0:T(8,128)} async-done(((f32[1,64,1024]{2,1,0:T(8,128)}), f32[16,64,1024]{2,1,0:T(8,128)}) %all-gather.4.cloned.1.call-update) | async-done | bytes 4194320 | tf_op jit(solution)/shard_map/all_gather | solution.py:41
  66.2 75.0 %all-gather.6.cloned.1.call-done = f32[32,64,1024]{2,1,0:T(8,128)} async-done(((f32[2,64,1024]{2,1,0:T(8,128)}), f32[32,64,1024]{2,1,0:T(8,128)}) %all-gather.6.cloned.1.call-update) | async-done | bytes 8388624 | tf_op jit(solution)/shard_map/all_gather | solution.py:41
  141.3 35.1 %while.26 = (s32[]{:T(128)}, f32[64,1024]{1,0:T(8,128)S(1)}, f32[2,64,1024]{2,1,0:T(8,128)S(1)}, s32[]{:T(128)}, f32[16,64,1024]{2,1,0:T(8,128)}, /*index=5*/f32...) while((s32[]{:T(128)}, f32[64,1024]{1,0:T(8,128)S(1)}, f32[2,64,1024]{2,1,0:T(8,128)S(1)}, ...), condition=%wide.region_2.3_spmd, body=%wide.region_1.2_spmd.sunk | while | flops 327686 | bytes 2883747 | solution.py:50
  177.4 1.4 add_divide_fusion
  179.7 3.4 %collective-permute-start.6 = (f32[4,1024]{1,0:T(4,128)S(1)}, f32[4,1024]{1,0:T(4,128)S(1)}, u32[]{:S(2)}, u32[]{:S(2)}) collective-permute-start(f32[4,1024]{1,0:T(4,128)S(1)} %get-tuple-element.191), channel_id=1, source_target_pairs={{0,1},{2,3},{4,5},{6,7},{8,9},{10,11},{12,13},{14,15},{16,17},{18,... | collective-permute-start | bytes 49160 | tf_op jit(solution)/shard_map/ppermute | solution.py:23
  183.1 1.3 collective-permute-start.5
  184.5 4.2 %collective-permute-done.5 = f32[4,1024]{1,0:T(4,128)S(1)} collective-permute-done((f32[4,1024]{1,0:T(4,128)S(1)}, f32[4,1024]{1,0:T(4,128)S(1)}, u32[]{:S(2)}, u32[]{:S(2)}) %collective-permute-start.5) | collective-permute-done | bytes 16416 | tf_op jit(solution)/shard_map/ppermute | solution.py:25
  189.8 29.7 %psum.14 = f32[32]{0:T(128)S(1)} all-reduce(f32[32]{0:T(128)S(1)} %select_reduce_fusion), channel_id=1, replica_groups=mesh['tm'=16,'strip'=2] {'tm'}, use_global_device_ids=true, to_apply=%region_7.8 | all-reduce | flops 32 | bytes 256 | tf_op jit(solution)/shard_map/psum | solution.py:143
  219.5 6.0 %psum.15 = f32[32]{0:T(128)} all-reduce(f32[32]{0:T(128)S(1)} %psum.14), channel_id=1, replica_groups=mesh['tm'=16,'strip'=2] {'strip'}, use_global_device_ids=true, to_apply=%region_8.9 | all-reduce | flops 32 | bytes 256 | tf_op jit(solution)/shard_map/psum | solution.py:143
  225.5 1.7 fusion.84
  228.0 3.9 %collective-permute-start.8 = (f32[4,1024]{1,0:T(4,128)S(1)}, f32[4,1024]{1,0:T(4,128)S(1)}, u32[]{:S(2)}, u32[]{:S(2)}) collective-permute-start(f32[4,1024]{1,0:T(4,128)S(1)} %get-tuple-element.177), channel_id=1, source_target_pairs={{0,1},{2,3},{4,5},{6,7},{8,9},{10,11},{12,13},{14,15},{16,17},{18,... | collective-permute-start | bytes 49160 | tf_op jit(solution)/shard_map/ppermute | solution.py:23
  232.0 1.3 collective-permute-start.7
  233.4 4.2 %collective-permute-done.7 = f32[4,1024]{1,0:T(4,128)S(1)} collective-permute-done((f32[4,1024]{1,0:T(4,128)S(1)}, f32[4,1024]{1,0:T(4,128)S(1)}, u32[]{:S(2)}, u32[]{:S(2)}) %collective-permute-start.7) | collective-permute-done | bytes 16416 | tf_op jit(solution)/shard_map/ppermute | solution.py:25
  237.6 2.2 fusion.9
  (111 shorter events, 51.9 us)
Async XLA Ops:
  7.2 59.0 %all-gather.4.cloned.1.call-start = ((), (), s32[]{:S(2)}) async-start(), calls=%async_computation | async-start | bytes 4456448 | tf_op jit(solution)/shard_map/all_gather | solution.py:41
  9.0 38.5 %copy-start = (f32[64,1024]{1,0:T(8,128)S(1)}, f32[64,1024]{1,0:T(8,128)}, u32[]{:S(2)}) copy-start(f32[64,1024]{1,0:T(8,128)} %param.13) | copy-start | bytes 786436
  9.0 132.2 %all-gather.6.cloned.1.call-start = ((), (), s32[]{:S(2)}) async-start(), calls=%async_computation.1 | async-start | bytes 8912896 | tf_op jit(solution)/shard_map/all_gather | solution.py:41
  9.9 23.5 %collective-permute-start.1 = (f32[4,1024]{1,0:T(4,128)S(1)}, f32[4,1024]{1,0:T(4,128)S(1)}, u32[]{:S(2)}, u32[]{:S(2)}) collective-permute-start(f32[4,1024]{1,0:T(4,128)S(1)} %get-tuple-element.229), channel_id=1, source_target_pairs={{0,1},{2,3},{4,5},{6,7},{8,9},{10,11},{12,13},{14,15},{16,17},{18,... | collective-permute-start | bytes 49160 | tf_op jit(solution)/shard_map/ppermute | solution.py:23
  14.7 18.7 %collective-permute-start = (f32[4,1024]{1,0:T(4,128)S(1)}, f32[4,1024]{1,0:T(4,128)S(1)}, u32[]{:S(2)}, u32[]{:S(2)}) collective-permute-start(f32[4,1024]{1,0:T(4,128)S(1)} %get-tuple-element.228), channel_id=1, source_target_pairs={{1,0},{3,2},{5,4},{7,6},{9,8},{11,10},{13,12},{15,14},{17,16},{19,... | collective-permute-start | bytes 49160 | tf_op jit(solution)/shard_map/ppermute | solution.py:25
  17.9 30.3 %collective-permute-start.4 = (f32[2,64,1024]{2,1,0:T(8,128)}, f32[2,64,1024]{2,1,0:T(8,128)S(1)}, u32[]{:S(2)}, u32[]{:S(2)}) collective-permute-start(f32[2,64,1024]{2,1,0:T(8,128)} %pad_maximum_fusion), channel_id=1, source_target_pairs={{0,30},{2,0},{4,2},{6,4},{8,6},{10,8},{12,10},{14,12},{16,14},{18,... | collective-permute-start | bytes 1572872 | tf_op jit(solution)/shard_map/ppermute | solution.py:34
  37.5 6.4 %collective-permute-start.3 = (f32[4,1024]{1,0:T(4,128)S(1)}, f32[4,1024]{1,0:T(4,128)S(1)}, u32[]{:S(2)}, u32[]{:S(2)}) collective-permute-start(f32[4,1024]{1,0:T(4,128)S(1)} %get-tuple-element.211), channel_id=1, source_target_pairs={{0,1},{2,3},{4,5},{6,7},{8,9},{10,11},{12,13},{14,15},{16,17},{18,... | collective-permute-start | bytes 49160 | tf_op jit(solution)/shard_map/ppermute | solution.py:23
  41.8 5.6 %collective-permute-start.2 = (f32[4,1024]{1,0:T(4,128)S(1)}, f32[4,1024]{1,0:T(4,128)S(1)}, u32[]{:S(2)}, u32[]{:S(2)}) collective-permute-start(f32[4,1024]{1,0:T(4,128)S(1)} %get-tuple-element.210), channel_id=1, source_target_pairs={{1,0},{3,2},{5,4},{7,6},{9,8},{11,10},{13,12},{15,14},{17,16},{19,... | collective-permute-start | bytes 49160 | tf_op jit(solution)/shard_map/ppermute | solution.py:25
  48.2 93.0 %copy-start.1 = (f32[2,64,1024]{2,1,0:T(8,128)}, f32[2,64,1024]{2,1,0:T(8,128)S(1)}, u32[]{:S(2)}) copy-start(f32[2,64,1024]{2,1,0:T(8,128)S(1)} %collective-permute-done.4) | copy-start | bytes 1572868
  176.4 1.0 copy-start.3
  176.5 12.2 %copy-start.2 = (f32[64,1024]{1,0:T(8,128)S(1)}, f32[64,1024]{1,0:T(8,128)}, u32[]{:S(2)}) copy-start(f32[64,1024]{1,0:T(8,128)} %get-tuple-element.156) | copy-start | bytes 786436
  176.5 13.2 %copy-start.4 = (s32[1,8]{1,0:T(1,128)S(1)}, s32[1,8]{1,0:T(1,128)}, u32[]{:S(2)}) copy-start(s32[1,8]{1,0:T(1,128)} %param.16) | copy-start | bytes 100
  179.7 4.8 %collective-permute-start.6 = (f32[4,1024]{1,0:T(4,128)S(1)}, f32[4,1024]{1,0:T(4,128)S(1)}, u32[]{:S(2)}, u32[]{:S(2)}) collective-permute-start(f32[4,1024]{1,0:T(4,128)S(1)} %get-tuple-element.191), channel_id=1, source_target_pairs={{0,1},{2,3},{4,5},{6,7},{8,9},{10,11},{12,13},{14,15},{16,17},{18,... | collective-permute-start | bytes 49160 | tf_op jit(solution)/shard_map/ppermute | solution.py:23
  183.1 5.6 %collective-permute-start.5 = (f32[4,1024]{1,0:T(4,128)S(1)}, f32[4,1024]{1,0:T(4,128)S(1)}, u32[]{:S(2)}, u32[]{:S(2)}) collective-permute-start(f32[4,1024]{1,0:T(4,128)S(1)} %get-tuple-element.190), channel_id=1, source_target_pairs={{1,0},{3,2},{5,4},{7,6},{9,8},{11,10},{13,12},{15,14},{17,16},{19,... | collective-permute-start | bytes 49160 | tf_op jit(solution)/shard_map/ppermute | solution.py:25
  184.4 41.1 %collective-permute-start.9 = (f32[2,64,1024]{2,1,0:T(8,128)S(1)}, f32[2,64,1024]{2,1,0:T(8,128)}, u32[]{:S(2)}, u32[]{:S(2)}) collective-permute-start(f32[2,64,1024]{2,1,0:T(8,128)S(1)} %add_divide_fusion), channel_id=1, source_target_pairs={{0,2},{2,4},{4,6},{6,8},{8,10},{10,12},{12,14},{14,16},{16,18},{18... | collective-permute-start | bytes 1572872 | tf_op jit(solution)/shard_map/ppermute | solution.py:34
  228.0 5.4 %collective-permute-start.8 = (f32[4,1024]{1,0:T(4,128)S(1)}, f32[4,1024]{1,0:T(4,128)S(1)}, u32[]{:S(2)}, u32[]{:S(2)}) collective-permute-start(f32[4,1024]{1,0:T(4,128)S(1)} %get-tuple-element.177), channel_id=1, source_target_pairs={{0,1},{2,3},{4,5},{6,7},{8,9},{10,11},{12,13},{14,15},{16,17},{18,... | collective-permute-start | bytes 49160 | tf_op jit(solution)/shard_map/ppermute | solution.py:23
  232.0 5.6 %collective-permute-start.7 = (f32[4,1024]{1,0:T(4,128)S(1)}, f32[4,1024]{1,0:T(4,128)S(1)}, u32[]{:S(2)}, u32[]{:S(2)}) collective-permute-start(f32[4,1024]{1,0:T(4,128)S(1)} %get-tuple-element.176), channel_id=1, source_target_pairs={{1,0},{3,2},{5,4},{7,6},{9,8},{11,10},{13,12},{15,14},{17,16},{19,... | collective-permute-start | bytes 49160 | tf_op jit(solution)/shard_map/ppermute | solution.py:25
Sparse Core Ops, SparseCore 0:
  10.1 56.0 all-gather.3
  68.4 72.8 all-gather.5
